TPU v7x, 32 devices: a whole 2x2x4 slice. The times are simulated.
32 devices in a mesh: leaf: 8 (over z, y), row: 4 (over x, core).
Axes of the slice: x: 2, y: 2, z: 4, core: 2. Of those that a mesh axis runs over, the one named last changes fastest.
Arguments:
- rhs_blocks: float32 [7, 1024, 256], P(None, 'leaf'), may hold values from -6 to 6
- diag_inverse: float32 [7, 1024, 1024], P(None, 'leaf', 'row'), may hold values from -0.1875 to 0.1875
- lower_blocks: float32 [6, 1024, 1024], P(None, 'leaf', 'row'), may hold values from -0.09375 to 0.09375
- update_rows: int32 [6, 1024], P(None, 'leaf'), may hold values from 512 to 895, as said below
Outputs:
- solution: float32 [7, 1024, 256], P(None, 'leaf')
Inputs may be any that keep to these rules, and one draw needn't show every extreme that they name: update_rows[s, m] = a * 128 + c names column i * 128 + c of an ancestor a of supernode s, where i = m // 128; the 128 entries of one supernode with the same i are distinct.
All inputs are finite; a program needn't handle non-finite values.
Results may differ from a plain program's by a relative error of at most 0.0001.
Values sent between devices are 32-bit elements; how exact they have to be, the bound alone decides.
No kernel may reach another device: no remote copies, remote signals or barrier semaphores. Data moves between devices by JAX's collectives and lax.ppermute only.
A program may use at most 64 MiB of HBM per device.

v0:
```python
import jax
import jax.numpy as jnp
from jax import lax
from jax.sharding import PartitionSpec as P


def local(rhs_blocks, diag_inverse, lower_blocks, update_rows):
    leaf_count = lax.axis_size("leaf")
    node_total = rhs_blocks.shape[0]
    panel_rows = rhs_blocks.shape[1]
    rhs_width = rhs_blocks.shape[2]
    level_total = (node_total + 1).bit_length() - 1
    slice_rows = diag_inverse.shape[2] // leaf_count
    current = rhs_blocks.reshape(node_total * panel_rows, rhs_width)
    stored_slices = [None] * level_total
    for depth_level in range(level_total - 1, -1, -1):
        first_node = 2**level_total - 2 ** (depth_level + 1)
        node_count = 2**depth_level
        stop_node = first_node + node_count
        diag_part = diag_inverse[first_node:stop_node]
        lower_part = lower_blocks[first_node:stop_node] if depth_level > 0 else None
        local_rhs = current[first_node * panel_rows : stop_node * panel_rows].reshape(
            node_count, panel_rows, rhs_width
        )
        partial_value = jnp.einsum(
            "scr,sct->rst", diag_part, local_rhs, precision=lax.Precision.HIGHEST
        )
        complete = lax.psum(partial_value, "leaf")
        stored = lax.dynamic_slice_in_dim(
            complete, lax.axis_index("leaf") * slice_rows, slice_rows, 0
        )
        if depth_level > 0:
            update = jnp.einsum(
                "smr,rst->smt", lower_part, complete, precision=lax.Precision.HIGHEST
            )
        stored_slices[depth_level] = stored
        if depth_level > 0:
            update = lax.psum(update, "row")
            targets = update_rows[first_node:stop_node].reshape(-1)
            current = current.at[targets].add(-update.reshape(-1, rhs_width))
    answer = jnp.zeros((node_total * panel_rows, rhs_width), jnp.float32)
    for depth_level in range(level_total):
        first_node = 2**level_total - 2 ** (depth_level + 1)
        node_count = 2**depth_level
        stop_node = first_node + node_count
        diag_part = diag_inverse[first_node:stop_node]
        residual = stored_slices[depth_level]
        if depth_level > 0:
            lower_part = lower_blocks[first_node:stop_node]
            targets = update_rows[first_node:stop_node].reshape(-1)
            known = answer[targets].reshape(node_count, panel_rows, rhs_width)
            residual = residual - lax.psum_scatter(
                jnp.einsum("smr,smt->rst", lower_part, known, precision=lax.Precision.HIGHEST),
                "leaf",
                scatter_dimension=0,
                tiled=True,
            )
        partial_value = jnp.einsum(
            "scr,rst->sct",
            diag_part,
            lax.all_gather(residual, "leaf", axis=0, tiled=True),
            precision=lax.Precision.HIGHEST,
        )
        solved = lax.psum(partial_value, "row")
        answer = answer.at[first_node * panel_rows : stop_node * panel_rows].set(
            solved.reshape(-1, rhs_width)
        )
    return answer.reshape(node_total, panel_rows, rhs_width)


def solution(mesh):
    placed = (
        P(None, "leaf", None),
        P(None, "leaf", "row"),
        P(None, "leaf", "row"),
        P(None, "leaf"),
    )
    return jax.shard_map(
        local, mesh=mesh, in_specs=placed, out_specs=P(None, "leaf", None), check_vma=False
    )
```

profile of v0, /device:TPU:0, one launch (start us, length us, event | category | flops | bytes accessed | tf_op | source)
XLA Modules:
  0.0 698.2 jit_solution(705623157416841822)
XLA Ops:
  6.5 1.3 copy.104
  8.0 2.0 convolution_bitcast_fusion.1
  10.1 81.5 %all-reduce.14.cloned.1.call-done = f32[256,4,256]{2,0,1:T(8,128)} async-done(((f32[256,4,256]{2,0,1:T(8,128)}), f32[256,4,256]{2,0,1:T(8,128)}) %all-reduce.14.cloned.1.call-update) | async-done | bytes 1048592 | tf_op jit(solution)/shard_map/psum | solution.py:28
  91.6 3.9 convolution_bitcast_fusion.4
  95.6 0.6 slice-done
  96.2 32.2 %all-reduce.16.cloned.1.call-done = f32[4,128,256]{1,2,0:T(8,128)} async-done(((f32[4,128,256]{1,2,0:T(8,128)}), f32[4,128,256]{1,2,0:T(8,128)}) %all-reduce.16.cloned.1.call-update) | async-done | bytes 524304 | tf_op jit(solution)/shard_map/psum | solution.py:38
  128.4 1.9 neg.12
  130.3 1.2 copy.47
  131.6 3.7 scatter_fusion
  135.3 1.4 convolution_bitcast_fusion.3
  136.8 0.6 copy-done.3
  137.4 71.9 %all-reduce.18.cloned.1.call-done = f32[256,2,256]{2,0,1:T(8,128)} async-done(((f32[256,2,256]{2,0,1:T(8,128)}), f32[256,2,256]{2,0,1:T(8,128)}) %all-reduce.18.cloned.1.call-update) | async-done | bytes 524304 | tf_op jit(solution)/shard_map/psum | solution.py:28
  209.3 2.8 convolution_bitcast_fusion.5
  212.1 31.3 %all-reduce.20.cloned.1.call-done = f32[2,128,256]{1,2,0:T(8,128)} async-done(((f32[2,128,256]{1,2,0:T(8,128)}), f32[2,128,256]{1,2,0:T(8,128)}) %all-reduce.20.cloned.1.call-update) | async-done | bytes 262160 | tf_op jit(solution)/shard_map/psum | solution.py:38
  243.5 1.0 neg.14
  244.6 2.3 scatter_fusion.1
  246.9 1.1 convolution_bitcast_fusion.6
  248.1 70.6 %all-reduce.22.cloned.1.call-done = f32[256,1,256]{0,2,1:T(8,128)} async-done(((f32[256,1,256]{0,2,1:T(8,128)}), f32[256,1,256]{0,2,1:T(8,128)}) %all-reduce.22.cloned.1.call-update) | async-done | bytes 262160 | tf_op jit(solution)/shard_map/psum | solution.py:28
  318.8 1.0 constant_dynamic-slice_fusion
  319.8 30.8 %all_gather.9 = f32[256,1,256]{2,1,0:T(1,128)S(1)} all-gather(f32[32,1,256]{2,1,0:T(1,128)S(1)} %copy.52), channel_id=1, replica_groups=mesh['leaf'=8,'row'=4] {'leaf'}, dimensions={0}, use_global_device_ids=true | all-gather | bytes 294912 | tf_op jit(solution)/shard_map/all_gather | solution.py:61
  350.6 1.3 convolution_bitcast_fusion.7
  352.0 30.8 %all-reduce.24.cloned.1.call-done = f32[128,256]{0,1:T(8,128)} async-done(((f32[128,256]{0,1:T(8,128)}), f32[128,256]{0,1:T(8,128)}) %all-reduce.24.cloned.1.call-update) | async-done | bytes 131088 | tf_op jit(solution)/shard_map/psum | solution.py:64
  382.8 1.0 scatter.10
  384.1 1.7 gather_fusion
  385.7 1.6 convolution_bitcast_fusion.2
  387.3 1.0 copy.55
  388.4 0.6 copy-done.4
  389.0 0.6 dynamic-slice.20
  390.3 70.6 %all-reduce.30.cloned.1.call-done = f32[256,2,256]{2,1,0:T(2,128)} async-done(((f32[256,2,256]{2,1,0:T(2,128)}), f32[256,2,256]{2,1,0:T(2,128)}) %all-reduce.30.cloned.1.call-update) | async-done | bytes 524304
  460.9 0.8 constant_dynamic-slice_fusion.2
  461.7 0.8 copy_subtract_fusion.1
  462.6 31.8 %all_gather.10 = f32[256,2,256]{2,1,0:T(2,128)S(1)} all-gather(f32[32,2,256]{2,1,0:T(2,128)S(1)} %copy.57), channel_id=1, replica_groups=mesh['leaf'=8,'row'=4] {'leaf'}, dimensions={0}, use_global_device_ids=true | all-gather | bytes 589824 | tf_op jit(solution)/shard_map/all_gather | solution.py:61
  494.8 0.8 copy.75
  495.8 31.2 %all-reduce.26.cloned.1.call-done = f32[256,256]{0,1:T(8,128)} async-done(((f32[256,256]{0,1:T(8,128)}), f32[256,256]{0,1:T(8,128)}) %all-reduce.26.cloned.1.call-update) | async-done | bytes 262160 | tf_op jit(solution)/shard_map/psum | solution.py:64
  527.0 1.0 constant_dynamic-update-slice_fusion.1
  528.3 1.6 gather_fusion.1
  529.8 2.1 convolution_bitcast_fusion
  531.9 1.3 copy.62
  533.3 78.3 %all-reduce.32.cloned.1.call-done = f32[256,4,256]{2,1,0:T(4,128)} async-done(((f32[256,4,256]{2,1,0:T(4,128)}), f32[256,4,256]{2,1,0:T(4,128)}) %all-reduce.32.cloned.1.call-update) | async-done | bytes 1048592
  611.6 0.9 constant_dynamic-slice_fusion.1
  612.5 0.9 copy_subtract_fusion
  613.5 0.7 copy.64
  614.3 39.8 %all-gather.2.cloned.1.call-done = f32[256,4,256]{2,1,0:T(4,128)} async-done(((f32[32,4,256]{2,1,0:T(4,128)}), f32[256,4,256]{2,1,0:T(4,128)}) %all-gather.2.cloned.1.call-update) | async-done | bytes 1048592 | tf_op jit(solution)/shard_map/all_gather | solution.py:61
  654.1 2.1 fusion
  656.2 1.0 copy.76
  657.3 32.1 %all-reduce.28.cloned.1.call-done = f32[512,256]{0,1:T(8,128)} async-done(((f32[512,256]{0,1:T(8,128)}), f32[512,256]{0,1:T(8,128)}) %all-reduce.28.cloned.1.call-update) | async-done | bytes 524304 | tf_op jit(solution)/shard_map/psum | solution.py:64
  689.3 1.1 constant_dynamic-update-slice_fusion
  690.4 1.2 copy.67
  (43 shorter events, 2.2 us)
Async XLA Ops:
  6.5 1.5 copy-start
  6.5 85.1 %all-reduce.14.cloned.1.call-start = ((), (), s32[]{:S(2)}) async-start(), calls=%async_computation | async-start | bytes 2097152 | tf_op jit(solution)/shard_map/psum | solution.py:28
  10.0 81.6 %copy-start.2 = (f32[6,128,256]{2,1,0:T(8,128)S(1)}, f32[6,128,256]{2,1,0:T(8,128)}, u32[]{:S(2)}) copy-start(f32[6,128,256]{2,1,0:T(8,128)} %param.12) | copy-start | bytes 2359300
  10.1 118.4 %all-reduce.16.cloned.1.call-start = ((), (), s32[]{:S(2)}) async-start(), calls=%async_computation.1 | async-start | bytes 1048576 | tf_op jit(solution)/shard_map/psum | solution.py:38
  95.5 0.7 slice-start
  95.5 113.7 %all-reduce.18.cloned.1.call-start = ((), (), s32[]{:S(2)}) async-start(), calls=%async_computation.2 | async-start | bytes 1048576 | tf_op jit(solution)/shard_map/psum | solution.py:28
  136.7 0.7 copy-start.3
  136.7 106.8 %all-reduce.20.cloned.1.call-start = ((), (), s32[]{:S(2)}) async-start(), calls=%async_computation.3 | async-start | bytes 524288 | tf_op jit(solution)/shard_map/psum | solution.py:38
  212.1 106.7 %all-reduce.22.cloned.1.call-start = ((), (), s32[]{:S(2)}) async-start(), calls=%async_computation.4 | async-start | bytes 524288 | tf_op jit(solution)/shard_map/psum | solution.py:28
  248.0 134.7 %all-reduce.24.cloned.1.call-start = ((), (), s32[]{:S(2)}) async-start(), calls=%async_computation.5 | async-start | bytes 262144 | tf_op jit(solution)/shard_map/psum | solution.py:64
  351.9 108.9 %all-reduce.30.cloned.1.call-start = ((), (), s32[]{:S(2)}) async-start(), calls=%async_computation.9 | async-start | bytes 1048576
  388.3 138.7 %all-reduce.26.cloned.1.call-start = ((), (), s32[]{:S(2)}) async-start(), calls=%async_computation.6 | async-start | bytes 524288 | tf_op jit(solution)/shard_map/psum | solution.py:64
  388.4 0.7 copy-start.4
  495.7 115.9 %all-reduce.32.cloned.1.call-start = ((), (), s32[]{:S(2)}) async-start(), calls=%async_computation.10 | async-start | bytes 2097152
  533.2 120.9 %copy-start.1 = (f32[7,128,256]{2,1,0:T(8,128)S(1)}, f32[7,128,256]{2,1,0:T(8,128)}, u32[]{:S(2)}) copy-start(f32[7,128,256]{2,1,0:T(8,128)} %param.11) | copy-start | bytes 2752516
  533.3 120.9 %all-gather.2.cloned.1.call-start = ((), (), s32[]{:S(2)}) async-start(), calls=%async_computation.7 | async-start | bytes 1179648 | tf_op jit(solution)/shard_map/all_gather | solution.py:61
  614.2 75.1 %all-reduce.28.cloned.1.call-start = ((), (), s32[]{:S(2)}) async-start(), calls=%async_computation.8 | async-start | bytes 1048576 | tf_op jit(solution)/shard_map/psum | solution.py:64
Sparse Core Ops, SparseCore 0:
  10.9 80.7 all-reduce.13
  95.6 32.7 all-reduce.15
  136.8 72.3 all-reduce.17
  212.2 31.2 all-reduce.19
  248.2 70.5 all-reduce.21
  352.0 30.6 all-reduce.23
  388.4 72.3 all-reduce.29
  495.8 31.1 all-reduce.25
  533.4 78.1 all-reduce.31
  614.4 39.7 all-gather.1
  657.4 31.8 all-reduce.27
where the time goes:
time: 699 us; the launch traced here: 698 us
  waiting for transfers between devices  571 us (82%)
  blocking collectives  62.6 us (9%)
  local copies, waits for them, and re-layouts  21.2 us (3%)
  matrix products  18.7 us (3%)
  between operations  14.1 us (2%)
  other arithmetic  10.6 us (2%)
    psum x3, waiting for transfers between devices, local(): complete = lax.psum(partial_value, 'leaf')  224 us
    unnamed x13, waiting for transfers between devices  149 us
    psum x3, waiting for transfers between devices, local(): solved = lax.psum(partial_value, 'row')  94.1 us
    psum x2, waiting for transfers between devices, local(): update = lax.psum(update, 'row')  63.6 us
    all_gather x2, blocking collectives, local(): lax.all_gather(residual, 'leaf', axis=0, tiled=True)  62.6 us
    all_gather x1, waiting for transfers between devices, local(): lax.all_gather(residual, 'leaf', axis=0, tiled=True)  39.8 us
  transfers between devices with their start and end apart: 11, of which 11 were waited for; matrix products, arithmetic and copies ran while one was open for 0% of the time, Pallas kernels for 0%

commit v1 on v0

--- a/solution.py
+++ b/solution.py
@@ -55,12 +55,41 @@
                 scatter_dimension=0,
                 tiled=True,
             )
+        tmp = lax.axis_size("leaf")
+        u_next = lax.axis_index("leaf")
+        h_now, z2, response = (tmp, u_next, residual.shape[0])
+        rows = tuple(((dev_i, (dev_i + 1) % h_now) for dev_i in range(h_now)))
+        tray = tuple(((dev_i, (dev_i - 1) % h_now) for dev_i in range(h_now)))
+        block_out = h_now // 2
+        local_next = g_now = residual
         partial_value = jnp.einsum(
             "scr,rst->sct",
-            diag_part,
-            lax.all_gather(residual, "leaf", axis=0, tiled=True),
+            lax.dynamic_slice_in_dim(diag_part, z2 * response, residual.shape[0], axis=2),
+            residual,
             precision=lax.Precision.HIGHEST,
         )
+        for it in range(1, block_out + 1):
+            local_next = lax.ppermute(local_next, axis_name="leaf", perm=rows)
+            if it < h_now - block_out:
+                g_now = lax.ppermute(g_now, axis_name="leaf", perm=tray)
+                v_now = jnp.einsum(
+                    "scr,rst->sct",
+                    lax.dynamic_slice_in_dim(
+                        diag_part, (z2 + it) % h_now * response, g_now.shape[0], axis=2
+                    ),
+                    g_now,
+                    precision=lax.Precision.HIGHEST,
+                )
+                partial_value = partial_value + v_now
+            base_arr = jnp.einsum(
+                "scr,rst->sct",
+                lax.dynamic_slice_in_dim(
+                    diag_part, (z2 - it) % h_now * response, local_next.shape[0], axis=2
+                ),
+                local_next,
+                precision=lax.Precision.HIGHEST,
+            )
+            partial_value = partial_value + base_arr
         solved = lax.psum(partial_value, "row")
         answer = answer.at[first_node * panel_rows : stop_node * panel_rows].set(
             solved.reshape(-1, rhs_width)

time: 699 us -> 758 us (1.084)
  waiting for transfers between devices: 571 us -> 649 us
  blocking collectives: 62.6 us -> 0 us
  starting transfers between devices: 0.42 us -> 39.4 us
    ppermute x0 -> x21, waiting for transfers between devices: none -> 123 us  [the longest x12 93.5 us: local(): local_next = lax.ppermute(local_next, axis_name='leaf', perm=rows)]
    all_gather x2 -> x0, blocking collectives: 62.6 us -> none  [local(): lax.all_gather(residual, 'leaf', axis=0, tiled=True)]
    all_gather x1 -> x0, waiting for transfers between devices: 39.8 us -> none  [local(): lax.all_gather(residual, 'leaf', axis=0, tiled=True)]
    ppermute x0 -> x21, starting transfers between devices: none -> 38.9 us  [the longest x9 28 us: local(): g_now = lax.ppermute(g_now, axis_name='leaf', perm=tray)]
    dot_general x3 -> x24, matrix products: 3.81 us -> 13.3 us  [the longest x12 7.68 us: local(): jnp.einsum('scr,rst->sct', lax.dynamic_slice_in_dim(diag_part, (z2 - it)...]
    unnamed x13 -> x12, waiting for transfers between devices: 149 us -> 149 us
  transfers between devices with their start and end apart: 11 -> 31, of which waited for: 11 -> 24; matrix products, arithmetic and copies ran while one was open for 0% -> 1% of each run, Pallas kernels for 0% -> 0%
where the time goes in v1:
time: 758 us
  waiting for transfers between devices  649 us (86%)
  starting transfers between devices  39.4 us (5%)
  matrix products  25.9 us (3%)
  local copies, waits for them, and re-layouts  18.2 us (2%)
  between operations  14.8 us (2%)
  other arithmetic  10.2 us (1%)
    psum x3, waiting for transfers between devices, local(): complete = lax.psum(partial_value, 'leaf')  224 us
    unnamed x12, waiting for transfers between devices  149 us
    ppermute x12, waiting for transfers between devices, local(): local_next = lax.ppermute(local_next, axis_name='leaf', perm=rows)  93.5 us
    psum x3, waiting for transfers between devices, local(): solved = lax.psum(partial_value, 'row')  89.5 us
    psum x2, waiting for transfers between devices, local(): update = lax.psum(update, 'row')  63.6 us
    ppermute x9, waiting for transfers between devices, local(): g_now = lax.ppermute(g_now, axis_name='leaf', perm=tray)  29.7 us
    ppermute x9, starting transfers between devices, local(): g_now = lax.ppermute(g_now, axis_name='leaf', perm=tray)  28 us
  transfers between devices with their start and end apart: 31, of which 24 were waited for; matrix products, arithmetic and copies ran while one was open for 1% of the time, Pallas kernels for 0%

profile of v1, /device:TPU:0, one launch (start us, length us, event | category | flops | bytes accessed | tf_op | source)
XLA Modules:
  0.0 757.6 jit_solution(8676655858397974763)
XLA Ops:
  6.5 1.3 copy.171
  8.0 2.0 convolution_bitcast_fusion.1
  10.1 81.6 %all-reduce.14.cloned.1.call-done = f32[256,4,256]{0,2,1:T(8,128)} async-done(((f32[256,4,256]{0,2,1:T(8,128)}), f32[256,4,256]{0,2,1:T(8,128)}) %all-reduce.14.cloned.1.call-update) | async-done | bytes 1048592 | tf_op jit(solution)/shard_map/psum | solution.py:28
  91.6 3.1 convolution_bitcast_fusion.4
  95.4 32.2 %all-reduce.16.cloned.1.call-done = f32[4,128,256]{1,2,0:T(8,128)} async-done(((f32[4,128,256]{1,2,0:T(8,128)}), f32[4,128,256]{1,2,0:T(8,128)}) %all-reduce.16.cloned.1.call-update) | async-done | bytes 524304 | tf_op jit(solution)/shard_map/psum | solution.py:38
  127.7 1.9 neg.12
  130.8 3.7 scatter_fusion
  134.5 1.4 convolution_bitcast_fusion.3
  136.6 71.9 %all-reduce.18.cloned.1.call-done = f32[256,2,256]{0,2,1:T(8,128)} async-done(((f32[256,2,256]{0,2,1:T(8,128)}), f32[256,2,256]{0,2,1:T(8,128)}) %all-reduce.18.cloned.1.call-update) | async-done | bytes 524304 | tf_op jit(solution)/shard_map/psum | solution.py:28
  208.5 2.3 convolution_bitcast_fusion.5
  210.9 31.3 %all-reduce.20.cloned.1.call-done = f32[2,128,256]{1,2,0:T(8,128)} async-done(((f32[2,128,256]{1,2,0:T(8,128)}), f32[2,128,256]{1,2,0:T(8,128)}) %all-reduce.20.cloned.1.call-update) | async-done | bytes 262160 | tf_op jit(solution)/shard_map/psum | solution.py:38
  243.4 2.3 scatter_fusion.1
  247.0 70.5 %all-reduce.22.cloned.1.call-done = f32[256,1,256]{0,2,1:T(8,128)} async-done(((f32[256,1,256]{0,2,1:T(8,128)}), f32[256,1,256]{0,2,1:T(8,128)}) %all-reduce.22.cloned.1.call-update) | async-done | bytes 262160 | tf_op jit(solution)/shard_map/psum | solution.py:28
  318.6 2.6 collective-permute-start
  321.6 7.4 collective-permute-done.1
  329.0 4.7 collective-permute-start.2
  334.4 2.4 collective-permute-done.3
  337.9 4.0 collective-permute-start.4
  342.2 3.0 collective-permute-done.5
  345.9 7.0 collective-permute-done.6
  354.1 28.5 %all-reduce.24.cloned.1.call-done = f32[128,256]{1,0:T(8,128)} async-done(((f32[128,256]{1,0:T(8,128)}), f32[128,256]{1,0:T(8,128)}) %all-reduce.24.cloned.1.call-update) | async-done | bytes 131088 | tf_op jit(solution)/shard_map/psum | solution.py:93
  388.3 70.5 %all-reduce.30.cloned.1.call-done = f32[256,2,256]{2,1,0:T(2,128)} async-done(((f32[256,2,256]{2,1,0:T(2,128)}), f32[256,2,256]{2,1,0:T(2,128)}) %all-reduce.30.cloned.1.call-update) | async-done | bytes 524304
  459.9 2.7 collective-permute-start.7
  463.0 9.0 %collective-permute-done.7 = f32[32,2,256]{0,2,1:T(8,128)S(1)} collective-permute-done((f32[32,2,256]{0,2,1:T(8,128)S(1)}, f32[32,2,256]{0,2,1:T(8,128)S(1)}, u32[]{:S(2)}, u32[]{:S(2)}) %collective-permute-start.7) | collective-permute-done | bytes 65568 | tf_op jit(solution)/shard_map/ppermute | solution.py:74
  473.5 3.4 collective-permute-done.8
  476.9 2.4 collective-permute-start.10
  479.8 7.9 %collective-permute-done.10 = f32[32,2,256]{0,2,1:T(8,128)S(1)} collective-permute-done((f32[32,2,256]{0,2,1:T(8,128)S(1)}, f32[32,2,256]{0,2,1:T(8,128)S(1)}, u32[]{:S(2)}, u32[]{:S(2)}) %collective-permute-start.10) | collective-permute-done | bytes 65568 | tf_op jit(solution)/shard_map/ppermute | solution.py:72
  488.2 4.7 collective-permute-start.11
  493.3 5.4 collective-permute-done.12
  499.2 2.5 collective-permute-start.13
  502.2 6.3 collective-permute-done.13
  509.7 30.4 %all-reduce.26.cloned.1.call-done = f32[256,256]{1,0:T(8,128)} async-done(((f32[256,256]{1,0:T(8,128)}), f32[256,256]{1,0:T(8,128)}) %all-reduce.26.cloned.1.call-update) | async-done | bytes 262160 | tf_op jit(solution)/shard_map/psum | solution.py:93
  541.1 1.6 gather_fusion.1
  542.7 2.1 convolution_bitcast_fusion
  544.8 1.3 copy.102
  546.2 78.2 %all-reduce.32.cloned.1.call-done = f32[256,4,256]{2,1,0:T(4,128)} async-done(((f32[256,4,256]{2,1,0:T(4,128)}), f32[256,4,256]{2,1,0:T(4,128)}) %all-reduce.32.cloned.1.call-update) | async-done | bytes 1048592
  626.3 1.2 dynamic-slice_subtract_fusion
  627.6 3.0 collective-permute-start.14
  631.2 20.6 %collective-permute-done.14 = f32[32,4,256]{0,2,1:T(8,128)S(1)} collective-permute-done((f32[32,4,256]{0,2,1:T(8,128)S(1)}, f32[32,4,256]{0,2,1:T(8,128)S(1)}, u32[]{:S(2)}, u32[]{:S(2)}) %collective-permute-start.14) | collective-permute-done | bytes 131104 | tf_op jit(solution)/shard_map/ppermute | solution.py:74
  653.1 10.0 %collective-permute-done.15 = f32[32,4,256]{0,2,1:T(8,128)S(1)} collective-permute-done((f32[32,4,256]{0,2,1:T(8,128)S(1)}, f32[32,4,256]{0,2,1:T(8,128)S(1)}, u32[]{:S(2)}, u32[]{:S(2)}) %collective-permute-start.15) | collective-permute-done | bytes 131104 | tf_op jit(solution)/shard_map/ppermute | solution.py:72
  663.1 2.5 collective-permute-start.17
  666.3 13.4 %collective-permute-done.17 = f32[32,4,256]{0,2,1:T(8,128)S(1)} collective-permute-done((f32[32,4,256]{0,2,1:T(8,128)S(1)}, f32[32,4,256]{0,2,1:T(8,128)S(1)}, u32[]{:S(2)}, u32[]{:S(2)}) %collective-permute-start.17) | collective-permute-done | bytes 131104 | tf_op jit(solution)/shard_map/ppermute | solution.py:72
  680.3 4.8 collective-permute-start.18
  685.7 16.0 %collective-permute-done.19 = f32[32,4,256]{0,2,1:T(8,128)S(1)} collective-permute-done((f32[32,4,256]{0,2,1:T(8,128)S(1)}, f32[32,4,256]{0,2,1:T(8,128)S(1)}, u32[]{:S(2)}, u32[]{:S(2)}) %collective-permute-start.19) | collective-permute-done | bytes 131104 | tf_op jit(solution)/shard_map/ppermute | solution.py:72
  701.7 2.5 collective-permute-start.20
  705.5 11.3 %collective-permute-done.20 = f32[32,4,256]{0,2,1:T(8,128)S(1)} collective-permute-done((f32[32,4,256]{0,2,1:T(8,128)S(1)}, f32[32,4,256]{0,2,1:T(8,128)S(1)}, u32[]{:S(2)}, u32[]{:S(2)}) %collective-permute-start.20) | collective-permute-done | bytes 131104 | tf_op jit(solution)/shard_map/ppermute | solution.py:72
  716.8 1.4 convolution_add_fusion
  718.2 30.5 %all-reduce.28.cloned.1.call-done = f32[512,256]{1,0:T(8,128)} async-done(((f32[512,256]{1,0:T(8,128)}), f32[512,256]{1,0:T(8,128)}) %all-reduce.28.cloned.1.call-update) | async-done | bytes 524304 | tf_op jit(solution)/shard_map/psum | solution.py:93
  (104 shorter events, 32.0 us)
Async XLA Ops:
  6.5 1.5 copy-start.1
  6.5 85.1 %all-reduce.14.cloned.1.call-start = ((), (), s32[]{:S(2)}) async-start(), calls=%async_computation | async-start | bytes 2097152 | tf_op jit(solution)/shard_map/psum | solution.py:28
  10.0 81.6 %copy-start.2 = (f32[6,128,256]{2,1,0:T(8,128)S(1)}, f32[6,128,256]{2,1,0:T(8,128)}, u32[]{:S(2)}) copy-start(f32[6,128,256]{2,1,0:T(8,128)} %param.12) | copy-start | bytes 2359300
  10.0 117.6 %all-reduce.16.cloned.1.call-start = ((), (), s32[]{:S(2)}) async-start(), calls=%async_computation.1 | async-start | bytes 1048576 | tf_op jit(solution)/shard_map/psum | solution.py:38
  94.7 0.7 slice-start
  94.7 113.7 %all-reduce.18.cloned.1.call-start = ((), (), s32[]{:S(2)}) async-start(), calls=%async_computation.2 | async-start | bytes 1048576 | tf_op jit(solution)/shard_map/psum | solution.py:28
  135.9 0.7 copy-start.6
  135.9 106.3 %all-reduce.20.cloned.1.call-start = ((), (), s32[]{:S(2)}) async-start(), calls=%async_computation.3 | async-start | bytes 524288 | tf_op jit(solution)/shard_map/psum | solution.py:38
  210.8 106.7 %all-reduce.22.cloned.1.call-start = ((), (), s32[]{:S(2)}) async-start(), calls=%async_computation.4 | async-start | bytes 524288 | tf_op jit(solution)/shard_map/psum | solution.py:28
  246.8 135.8 %all-reduce.24.cloned.1.call-start = ((), (), s32[]{:S(2)}) async-start(), calls=%async_computation.5 | async-start | bytes 262144 | tf_op jit(solution)/shard_map/psum | solution.py:93
  317.5 3.7 copy-start.5
  318.6 10.4 %collective-permute-start = (f32[32,1,256]{0,2,1:T(8,128)S(1)}, f32[32,1,256]{0,2,1:T(8,128)S(1)}, u32[]{:S(2)}, u32[]{:S(2)}) collective-permute-start(f32[32,1,256]{0,2,1:T(8,128)S(1)} %constant_dynamic-slice_fusion), channel_id=1, source_target_pairs={{0,28},{4,0},{8,4},{12,8},{16,12},{20,16},{24,20},{28,24},{1,29},{... | collective-permute-start | bytes 98312 | tf_op jit(solution)/shard_map/ppermute | solution.py:74
  321.2 7.8 %collective-permute-start.1 = (f32[32,1,256]{0,2,1:T(8,128)S(1)}, f32[32,1,256]{0,2,1:T(8,128)S(1)}, u32[]{:S(2)}, u32[]{:S(2)}) collective-permute-start(f32[32,1,256]{0,2,1:T(8,128)S(1)} %constant_dynamic-slice_fusion), channel_id=1, source_target_pairs={{0,4},{4,8},{8,12},{12,16},{16,20},{20,24},{24,28},{28,0},{1,5},{5... | collective-permute-start | bytes 98312 | tf_op jit(solution)/shard_map/ppermute | solution.py:72
  329.0 7.8 %collective-permute-start.3 = (f32[32,1,256]{0,2,1:T(8,128)S(1)}, f32[32,1,256]{0,2,1:T(8,128)S(1)}, u32[]{:S(2)}, u32[]{:S(2)}) collective-permute-start(f32[32,1,256]{0,2,1:T(8,128)S(1)} %collective-permute-done.1), channel_id=1, source_target_pairs={{0,4},{4,8},{8,12},{12,16},{16,20},{20,24},{24,28},{28,0},{1,5},{5... | collective-permute-start | bytes 98312 | tf_op jit(solution)/shard_map/ppermute | solution.py:72
  329.0 8.9 %collective-permute-start.2 = (f32[32,1,256]{0,2,1:T(8,128)S(1)}, f32[32,1,256]{0,2,1:T(8,128)S(1)}, u32[]{:S(2)}, u32[]{:S(2)}) collective-permute-start(f32[32,1,256]{0,2,1:T(8,128)S(1)} %collective-permute-done), channel_id=1, source_target_pairs={{0,28},{4,0},{8,4},{12,8},{16,12},{20,16},{24,20},{28,24},{1,29},{... | collective-permute-start | bytes 98312 | tf_op jit(solution)/shard_map/ppermute | solution.py:74
  336.8 8.4 %collective-permute-start.5 = (f32[32,1,256]{0,2,1:T(8,128)S(1)}, f32[32,1,256]{0,2,1:T(8,128)S(1)}, u32[]{:S(2)}, u32[]{:S(2)}) collective-permute-start(f32[32,1,256]{0,2,1:T(8,128)S(1)} %collective-permute-done.3), channel_id=1, source_target_pairs={{0,4},{4,8},{8,12},{12,16},{16,20},{20,24},{24,28},{28,0},{1,5},{5... | collective-permute-start | bytes 98312 | tf_op jit(solution)/shard_map/ppermute | solution.py:72
  337.9 7.7 %collective-permute-start.4 = (f32[32,1,256]{0,2,1:T(8,128)S(1)}, f32[32,1,256]{0,2,1:T(8,128)S(1)}, u32[]{:S(2)}, u32[]{:S(2)}) collective-permute-start(f32[32,1,256]{0,2,1:T(8,128)S(1)} %collective-permute-done.2), channel_id=1, source_target_pairs={{0,28},{4,0},{8,4},{12,8},{16,12},{20,16},{24,20},{28,24},{1,29},{... | collective-permute-start | bytes 98312 | tf_op jit(solution)/shard_map/ppermute | solution.py:74
  345.2 7.7 %collective-permute-start.6 = (f32[32,1,256]{0,2,1:T(8,128)S(1)}, f32[32,1,256]{0,2,1:T(8,128)S(1)}, u32[]{:S(2)}, u32[]{:S(2)}) collective-permute-start(f32[32,1,256]{0,2,1:T(8,128)S(1)} %collective-permute-done.5), channel_id=1, source_target_pairs={{0,4},{4,8},{8,12},{12,16},{16,20},{20,24},{24,28},{28,0},{1,5},{5... | collective-permute-start | bytes 98312 | tf_op jit(solution)/shard_map/ppermute | solution.py:72
  353.9 104.9 %all-reduce.30.cloned.1.call-start = ((), (), s32[]{:S(2)}) async-start(), calls=%async_computation.8 | async-start | bytes 1048576
  386.2 73.5 %copy-start.4 = (f32[256,2,256]{0,2,1:T(8,128)S(1)}, f32[256,2,256]{0,2,1:T(8,128)}, u32[]{:S(2)}) copy-start(f32[256,2,256]{0,2,1:T(8,128)} %all-reduce.18.cloned.1.call-done) | copy-start | bytes 1572868
  386.3 153.9 %all-reduce.26.cloned.1.call-start = ((), (), s32[]{:S(2)}) async-start(), calls=%async_computation.6 | async-start | bytes 524288 | tf_op jit(solution)/shard_map/psum | solution.py:93
  386.3 0.7 copy-start.7
  459.9 12.2 %collective-permute-start.7 = (f32[32,2,256]{0,2,1:T(8,128)S(1)}, f32[32,2,256]{0,2,1:T(8,128)S(1)}, u32[]{:S(2)}, u32[]{:S(2)}) collective-permute-start(f32[32,2,256]{0,2,1:T(8,128)S(1)} %dynamic-slice_subtract_fusion.1), channel_id=1, source_target_pairs={{0,28},{4,0},{8,4},{12,8},{16,12},{20,16},{24,20},{28,24},{1,29},{... | collective-permute-start | bytes 196616 | tf_op jit(solution)/shard_map/ppermute | solution.py:74
  462.6 14.3 %collective-permute-start.8 = (f32[32,2,256]{0,2,1:T(8,128)S(1)}, f32[32,2,256]{0,2,1:T(8,128)S(1)}, u32[]{:S(2)}, u32[]{:S(2)}) collective-permute-start(f32[32,2,256]{0,2,1:T(8,128)S(1)} %dynamic-slice_subtract_fusion.1), channel_id=1, source_target_pairs={{0,4},{4,8},{8,12},{12,16},{16,20},{20,24},{24,28},{28,0},{1,5},{5... | collective-permute-start | bytes 196616 | tf_op jit(solution)/shard_map/ppermute | solution.py:72
  472.1 16.1 %collective-permute-start.9 = (f32[32,2,256]{0,2,1:T(8,128)S(1)}, f32[32,2,256]{0,2,1:T(8,128)S(1)}, u32[]{:S(2)}, u32[]{:S(2)}) collective-permute-start(f32[32,2,256]{0,2,1:T(8,128)S(1)} %collective-permute-done.7), channel_id=1, source_target_pairs={{0,28},{4,0},{8,4},{12,8},{16,12},{20,16},{24,20},{28,24},{1,29},{... | collective-permute-start | bytes 196616 | tf_op jit(solution)/shard_map/ppermute | solution.py:74
  476.9 10.8 %collective-permute-start.10 = (f32[32,2,256]{0,2,1:T(8,128)S(1)}, f32[32,2,256]{0,2,1:T(8,128)S(1)}, u32[]{:S(2)}, u32[]{:S(2)}) collective-permute-start(f32[32,2,256]{0,2,1:T(8,128)S(1)} %collective-permute-done.8), channel_id=1, source_target_pairs={{0,4},{4,8},{8,12},{12,16},{16,20},{20,24},{24,28},{28,0},{1,5},{5... | collective-permute-start | bytes 196616 | tf_op jit(solution)/shard_map/ppermute | solution.py:72
  488.1 10.7 %collective-permute-start.12 = (f32[32,2,256]{0,2,1:T(8,128)S(1)}, f32[32,2,256]{0,2,1:T(8,128)S(1)}, u32[]{:S(2)}, u32[]{:S(2)}) collective-permute-start(f32[32,2,256]{0,2,1:T(8,128)S(1)} %collective-permute-done.10), channel_id=1, source_target_pairs={{0,4},{4,8},{8,12},{12,16},{16,20},{20,24},{24,28},{28,0},{1,5},{5... | collective-permute-start | bytes 196616 | tf_op jit(solution)/shard_map/ppermute | solution.py:72
  488.2 13.5 %collective-permute-start.11 = (f32[32,2,256]{0,2,1:T(8,128)S(1)}, f32[32,2,256]{0,2,1:T(8,128)S(1)}, u32[]{:S(2)}, u32[]{:S(2)}) collective-permute-start(f32[32,2,256]{0,2,1:T(8,128)S(1)} %collective-permute-done.9), channel_id=1, source_target_pairs={{0,28},{4,0},{8,4},{12,8},{16,12},{20,16},{24,20},{28,24},{1,29},{... | collective-permute-start | bytes 196616 | tf_op jit(solution)/shard_map/ppermute | solution.py:74
  499.2 9.3 %collective-permute-start.13 = (f32[32,2,256]{0,2,1:T(8,128)S(1)}, f32[32,2,256]{0,2,1:T(8,128)S(1)}, u32[]{:S(2)}, u32[]{:S(2)}) collective-permute-start(f32[32,2,256]{0,2,1:T(8,128)S(1)} %collective-permute-done.12), channel_id=1, source_target_pairs={{0,4},{4,8},{8,12},{12,16},{16,20},{20,24},{24,28},{28,0},{1,5},{5... | collective-permute-start | bytes 196616 | tf_op jit(solution)/shard_map/ppermute | solution.py:72
  509.6 114.8 %all-reduce.32.cloned.1.call-start = ((), (), s32[]{:S(2)}) async-start(), calls=%async_computation.9 | async-start | bytes 2097152
  546.1 80.2 %copy-start.3 = (f32[256,4,256]{0,2,1:T(8,128)S(1)}, f32[256,4,256]{0,2,1:T(8,128)}, u32[]{:S(2)}) copy-start(f32[256,4,256]{0,2,1:T(8,128)} %all-reduce.14.cloned.1.call-done) | copy-start | bytes 3145732
  546.1 202.6 %all-reduce.28.cloned.1.call-start = ((), (), s32[]{:S(2)}) async-start(), calls=%async_computation.7 | async-start | bytes 1048576 | tf_op jit(solution)/shard_map/psum | solution.py:93
  627.6 24.3 %collective-permute-start.14 = (f32[32,4,256]{0,2,1:T(8,128)S(1)}, f32[32,4,256]{0,2,1:T(8,128)S(1)}, u32[]{:S(2)}, u32[]{:S(2)}) collective-permute-start(f32[32,4,256]{0,2,1:T(8,128)S(1)} %dynamic-slice_subtract_fusion), channel_id=1, source_target_pairs={{0,28},{4,0},{8,4},{12,8},{16,12},{20,16},{24,20},{28,24},{1,29},{... | collective-permute-start | bytes 393224 | tf_op jit(solution)/shard_map/ppermute | solution.py:74
  630.6 32.5 %collective-permute-start.15 = (f32[32,4,256]{0,2,1:T(8,128)S(1)}, f32[32,4,256]{0,2,1:T(8,128)S(1)}, u32[]{:S(2)}, u32[]{:S(2)}) collective-permute-start(f32[32,4,256]{0,2,1:T(8,128)S(1)} %dynamic-slice_subtract_fusion), channel_id=1, source_target_pairs={{0,4},{4,8},{8,12},{12,16},{16,20},{20,24},{24,28},{28,0},{1,5},{5... | collective-permute-start | bytes 393224 | tf_op jit(solution)/shard_map/ppermute | solution.py:72
  651.9 28.4 %collective-permute-start.16 = (f32[32,4,256]{0,2,1:T(8,128)S(1)}, f32[32,4,256]{0,2,1:T(8,128)S(1)}, u32[]{:S(2)}, u32[]{:S(2)}) collective-permute-start(f32[32,4,256]{0,2,1:T(8,128)S(1)} %collective-permute-done.14), channel_id=1, source_target_pairs={{0,28},{4,0},{8,4},{12,8},{16,12},{20,16},{24,20},{28,24},{1,29},{... | collective-permute-start | bytes 393224 | tf_op jit(solution)/shard_map/ppermute | solution.py:74
  663.1 16.5 %collective-permute-start.17 = (f32[32,4,256]{0,2,1:T(8,128)S(1)}, f32[32,4,256]{0,2,1:T(8,128)S(1)}, u32[]{:S(2)}, u32[]{:S(2)}) collective-permute-start(f32[32,4,256]{0,2,1:T(8,128)S(1)} %collective-permute-done.15), channel_id=1, source_target_pairs={{0,4},{4,8},{8,12},{12,16},{16,20},{20,24},{24,28},{28,0},{1,5},{5... | collective-permute-start | bytes 393224 | tf_op jit(solution)/shard_map/ppermute | solution.py:72
  679.7 22.0 %collective-permute-start.19 = (f32[32,4,256]{0,2,1:T(8,128)S(1)}, f32[32,4,256]{0,2,1:T(8,128)S(1)}, u32[]{:S(2)}, u32[]{:S(2)}) collective-permute-start(f32[32,4,256]{0,2,1:T(8,128)S(1)} %collective-permute-done.17), channel_id=1, source_target_pairs={{0,4},{4,8},{8,12},{12,16},{16,20},{20,24},{24,28},{28,0},{1,5},{5... | collective-permute-start | bytes 393224 | tf_op jit(solution)/shard_map/ppermute | solution.py:72
  680.3 24.5 %collective-permute-start.18 = (f32[32,4,256]{0,2,1:T(8,128)S(1)}, f32[32,4,256]{0,2,1:T(8,128)S(1)}, u32[]{:S(2)}, u32[]{:S(2)}) collective-permute-start(f32[32,4,256]{0,2,1:T(8,128)S(1)} %collective-permute-done.16), channel_id=1, source_target_pairs={{0,28},{4,0},{8,4},{12,8},{16,12},{20,16},{24,20},{28,24},{1,29},{... | collective-permute-start | bytes 393224 | tf_op jit(solution)/shard_map/ppermute | solution.py:74
  701.7 15.1 %collective-permute-start.20 = (f32[32,4,256]{0,2,1:T(8,128)S(1)}, f32[32,4,256]{0,2,1:T(8,128)S(1)}, u32[]{:S(2)}, u32[]{:S(2)}) collective-permute-start(f32[32,4,256]{0,2,1:T(8,128)S(1)} %collective-permute-done.19), channel_id=1, source_target_pairs={{0,4},{4,8},{8,12},{12,16},{16,20},{20,24},{24,28},{28,0},{1,5},{5... | collective-permute-start | bytes 393224 | tf_op jit(solution)/shard_map/ppermute | solution.py:72
  749.8 0.9 copy-start
Sparse Core Ops, SparseCore 0:
  10.9 80.7 all-reduce.13
  94.8 32.7 all-reduce.15
  136.0 72.3 all-reduce.17
  211.0 31.2 all-reduce.19
  246.9 70.5 all-reduce.21
  354.0 28.6 all-reduce.23
  386.5 72.2 all-reduce.29
  509.8 30.3 all-reduce.25
  546.2 78.1 all-reduce.31
  718.3 30.3 all-reduce.27
